TPU v7x, 32 devices: a whole 2x2x4 slice. The times are simulated.
32 devices in a mesh: tile: 8 (over y, x, core), aux: 4 (over z).
Axes of the slice: x: 2, y: 2, z: 4, core: 2. Of those that a mesh axis runs over, the one named last changes fastest.
Arguments:
- amps: bfloat16 [8, 8, 128, 128], P('tile'), may hold values from -6 to 6
- fitted: bfloat16 [2048, 8, 128], P('aux'), may hold values from -0.375 to 0.375
- screen: int32 [16, 8], P('aux'), may hold values 0 or 1
- owner: int32 [8], replicated, may hold values from 0 to 7, each once
- eps_occ: float32 [8], replicated, may hold values from -2 to -0.5
- eps_vir: float32 [128], replicated, may hold values from 0.5 to 2
Outputs:
- update: bfloat16 [8, 128, 8, 128], P(None, None, 'tile')
Inputs may be any that keep to these rules, and one draw needn't show every extreme that they name: owner is a permutation of the occupied orbitals.
All inputs are finite; a program needn't handle non-finite values. No bound on the sum of `screen` on one device may be relied on, other than what follows from the above.
Results may differ from a plain program's by a relative error of at most 0.0034.
Values may be sent and summed in bfloat16 or wider, within the bound.
No kernel may reach another device: no remote copies, remote signals or barrier semaphores. Data moves between devices by JAX's collectives and lax.ppermute only.
A program may use at most 64 MiB of HBM per device.

v0:
```python
import jax
import jax.numpy as jnp
from jax import lax
from jax.sharding import PartitionSpec as P


def on_device(amps, fitted, screen, owner, eps_occ, eps_vir):
    occ_dev = amps.shape[0]
    qblock_size = fitted.shape[0] // screen.shape[0]
    tile_mask = jnp.repeat(screen, qblock_size, axis=0).astype(jnp.bfloat16)
    screened = fitted * tile_mask[:, :, None]
    permuted = jnp.take(amps, owner, axis=1)
    received = lax.all_to_all(permuted, "tile", split_axis=1, concat_axis=0, tiled=True)
    intermed = jnp.einsum(
        "qkc,kpcb->qpb", screened, received, preferred_element_type=jnp.float32
    ).astype(jnp.bfloat16)
    partial_cycle = jnp.einsum(
        "qia,qpb->iapb", screened, intermed, preferred_element_type=jnp.float32
    )
    slot_start = lax.axis_index("tile") * occ_dev
    own_owner = lax.dynamic_slice_in_dim(owner, slot_start, occ_dev, 0)
    eps_slot = jnp.take(eps_occ, own_owner, axis=0)
    virt_pair = (
        eps_vir[None, :, None, None] + eps_vir[None, None, None, :] - eps_slot[None, None, :, None]
    )
    occ_rows = partial_cycle.shape[0]
    aux_count = lax.axis_size("aux")
    share_rows = -(-occ_rows // aux_count)
    extra_rows = share_rows * aux_count - occ_rows
    padded = jnp.pad(partial_cycle, ((0, extra_rows), (0, 0), (0, 0), (0, 0)))
    cycle_share = lax.psum_scatter(padded, "aux", scatter_dimension=0, tiled=True)
    eps_padded = jnp.pad(eps_occ, (0, extra_rows))
    eps_share = lax.dynamic_slice_in_dim(
        eps_padded, lax.axis_index("aux") * share_rows, share_rows, 0
    )
    denominator = virt_pair - eps_share[:, None, None, None]
    divided = (cycle_share / denominator).astype(jnp.bfloat16)
    gathered = lax.all_gather(divided, "aux", axis=0, tiled=True)
    return gathered[:occ_rows]


def solution(mesh):
    placed = (P("tile", None, None, None), P("aux", None, None), P("aux", None), P(), P(), P())
    return jax.shard_map(
        on_device,
        mesh=mesh,
        in_specs=placed,
        out_specs=P(None, None, "tile", None),
        check_vma=False,
    )
```

profile of v0, /device:TPU:0, one launch (start us, length us, event | category | flops | bytes accessed | tf_op | source)
XLA Modules:
  0.0 68.3 jit_solution(11172948436916942346)
XLA Ops:
  6.5 0.0 copy-start
  6.5 0.0 copy-start.4
  6.5 0.0 copy-start.1
  6.5 0.8 %compare_select_fusion = s32[8]{0:T(128)S(1)} fusion(s32[8]{0:T(128)} %param.9), kind=kLoop, calls=%fused_computation.12 | loop fusion | flops 24 | bytes 64 | tf_op jit(solution)/shard_map/jit(_take)/jit(_where)/select_n | solution.py:12
  7.3 0.0 copy-done.4
  7.3 0.2 copy-done
  7.5 0.6 gather_fusion
  8.1 0.8 %bitcast_select_fusion = bf16[1,8,128,128]{3,2,0,1:T(8,128)(2,1)} fusion(bf16[8,128,128]{2,1,0:T(8,128)(2,1)S(1)} %gather_fusion, pred[8]{0:T(512)(128)(4,1)S(1)} %compare_and_fusion), kind=kLoop, calls=%fused_computation.7 | loop fusion | flops 131072 | bytes 524296 | tf_op jit(solution)/shard_map/jit(_take)/select_n | solution.py:12
  8.9 0.0 copy-start.3
  8.9 5.3 %all-to-all-start = ((bf16[1,8,128,128]{3,2,0,1:T(8,128)(2,1)}), bf16[1,8,128,128]{3,2,0,1:T(8,128)(2,1)}, u32[]{:S(2)}, u32[]{:S(2)}) async-start(bf16[1,8,128,128]{3,2,0,1:T(8,128)(2,1)} %bitcast_select_fusion), calls=%async_computation | async-start | bytes 524288 | tf_op jit(solution)/shard_map/all_to_all | solution.py:13
  14.2 0.0 reduce-scatter.2.cloned.1.call-start
  14.3 0.0 copy-done.3
  14.3 0.0 copy-done.1
  14.3 0.7 %broadcast_multiply_fusion = bf16[512,8,128]{2,1,0:T(8,128)(2,1)S(1)} fusion(bf16[512,8,128]{2,1,0:T(8,128)(2,1)S(1)} %copy-done.1, bf16[512,8]{1,0:T(8,128)(2,1)S(1)} %bitcast.29), kind=kLoop, calls=%fused_computation.5 | loop fusion | flops 524288 | bytes 2105344 | tf_op jit(solution)/shard_map/mul | solution.py:11
  15.1 0.7 copy.9
  15.7 5.5 %all-to-all-done = bf16[1,8,128,128]{3,2,0,1:T(8,128)(2,1)} async-done(((bf16[1,8,128,128]{3,2,0,1:T(8,128)(2,1)}), bf16[1,8,128,128]{3,2,0,1:T(8,128)(2,1)}, u32[]{:S(2)}, u32[]{:S(2)}) %all-to-all-start) | async-done | bytes 262176 | tf_op jit(solution)/shard_map/all_to_all | solution.py:13
  21.2 3.1 %convolution_bitcast_fusion = f32[8,128,1,128]{3,1,0,2:T(8,128)} fusion(bf16[512,8,128]{0,2,1:T(8,128)(2,1)S(1)} %copy.9, bf16[1,8,128,128]{3,2,0,1:T(8,128)(2,1)} %all-to-all-done), kind=kOutput, calls=%fused_computation.1 | convolution fusion | flops 268500992 | bytes 1835008 | tf_op jit(solution)/shard_map/qia,qpb->iapb/dot_general | solution.py:17
  24.3 0.0 reduce-scatter.2.cloned.1.call-update
  24.3 0.6 dynamic_slice.6
  26.9 0.0 copy-start.5
  26.9 0.6 copy-done.5
  27.5 0.1 dynamic_slice.7
  27.6 0.6 dynamic-slice.2
  28.7 0.0 copy-start.2
  28.7 0.6 copy-done.2
  29.4 0.1 add_subtract_fusion
  29.4 16.5 %reduce-scatter.2.cloned.1.call-done = f32[2,128,1,128]{3,1,0,2:T(8,128)} async-done(((f32[8,128,1,128]{3,1,0,2:T(8,128)}), f32[2,128,1,128]{3,1,0,2:T(8,128)}) %reduce-scatter.2.cloned.1.call-update) | async-done | bytes 131088 | tf_op jit(solution)/shard_map/reduce_scatter | solution.py:31
  45.9 1.0 %fusion.4 = bf16[2,128,1,128]{3,1,2,0:T(8,128)(2,1)S(1)} fusion(f32[2,128,1,128]{3,1,0,2:T(8,128)} %reduce-scatter.2.cloned.1.call-done, f32[2]{0:T(128)S(1)} %dynamic_slice.7, f32[128,128]{1,0:T(8,128)S(1)} %add_subtract_fusion), kind=kLoop, calls=%fused_computation.10 | loop fusion | flops 98304 | bytes 262152 | tf_op jit(solution)/shard_map/convert_element_type | solution.py:37
  46.9 13.8 %all_gather.3 = bf16[8,128,1,128]{3,1,2,0:T(8,128)(2,1)S(1)} all-gather(bf16[2,128,1,128]{3,1,2,0:T(8,128)(2,1)S(1)} %fusion.4), channel_id=1, replica_groups=mesh['tile'=8,'aux'=4] {'aux'}, dimensions={0}, use_global_device_ids=true | all-gather | bytes 327680 | tf_op jit(solution)/shard_map/all_gather | solution.py:38
  60.7 0.7 %copy.13 = bf16[8,128,1,128]{3,1,2,0:T(8,128)(2,1)} copy(bf16[8,128,1,128]{3,1,2,0:T(8,128)(2,1)S(1)} %all_gather.3) | data formatting | bytes 524288
  (4 shorter events, 0.0 us)
Async XLA Ops:
  6.5 1.0 %copy-start = (bf16[1,8,128,128]{3,2,1,0:T(8,128)(2,1)S(1)}, bf16[1,8,128,128]{3,2,1,0:T(8,128)(2,1)}, u32[]{:S(2)}) copy-start(bf16[1,8,128,128]{3,2,1,0:T(8,128)(2,1)} %param.6) | copy-start | bytes 786436
  6.5 0.8 %copy-start.4 = (s32[8]{0:T(128)S(1)}, s32[8]{0:T(128)}, u32[]{:S(2)}) copy-start(s32[8]{0:T(128)} %param.9) | copy-start | bytes 100
  6.5 7.8 %copy-start.1 = (bf16[512,8,128]{2,1,0:T(8,128)(2,1)S(1)}, bf16[512,8,128]{2,1,0:T(8,128)(2,1)}, u32[]{:S(2)}) copy-start(bf16[512,8,128]{2,1,0:T(8,128)(2,1)} %param.7) | copy-start | bytes 3145732
  8.9 5.4 %copy-start.3 = (s32[4,8]{1,0:T(4,128)S(1)}, s32[4,8]{1,0:T(4,128)}, u32[]{:S(2)}) copy-start(s32[4,8]{1,0:T(4,128)} %param.8) | copy-start | bytes 388
  8.9 12.3 %all-to-all-start = ((bf16[1,8,128,128]{3,2,0,1:T(8,128)(2,1)}), bf16[1,8,128,128]{3,2,0,1:T(8,128)(2,1)}, u32[]{:S(2)}, u32[]{:S(2)}) async-start(bf16[1,8,128,128]{3,2,0,1:T(8,128)(2,1)} %bitcast_select_fusion), calls=%async_computation | async-start | bytes 524288 | tf_op jit(solution)/shard_map/all_to_all | solution.py:13
  14.2 31.7 %reduce-scatter.2.cloned.1.call-start = ((), (), s32[]{:S(2)}) async-start(), calls=%async_computation.2 | async-start | bytes 655360 | tf_op jit(solution)/shard_map/reduce_scatter | solution.py:31
  26.9 0.7 copy-start.5
  28.7 0.7 copy-start.2
Sparse Core Ops, SparseCore 0:
  24.4 21.4 reduce-scatter.1
where the time goes:
time: 68.6 us; the launch traced here: 68.3 us
  waiting for transfers between devices  22 us (32%)
  between operations  16 us (23%)
  blocking collectives  13.8 us (20%)
  starting transfers between devices  5.37 us (8%)
  local copies, waits for them, and re-layouts  4.7 us (7%)
  other arithmetic  3.36 us (5%)
  matrix products  3.05 us (4%)
    reduce_scatter x1, waiting for transfers between devices, on_device(): lax.psum_scatter(padded, 'aux', scatter_dimension=0, tiled=True)  16.5 us
    all_gather x1, blocking collectives, on_device(): gathered = lax.all_gather(divided, 'aux', axis=0, tiled=True)  13.8 us
    all_to_all x1, waiting for transfers between devices, on_device(): lax.all_to_all(permuted, 'tile', split_axis=1, concat_axis=0, tiled=True)  5.5 us
    all_to_all x1, starting transfers between devices, on_device(): lax.all_to_all(permuted, 'tile', split_axis=1, concat_axis=0, tiled=True)  5.33 us
    dot_general x1, matrix products, on_device(): jnp.einsum('qia,qpb->iapb', screened, intermed, preferred_element_type=jn...  3.05 us
    unnamed x13, local copies, waits for them, and re-layouts  2.19 us
    select_n x2, other arithmetic, on_device(): permuted = jnp.take(amps, owner, axis=1)  1.56 us
  transfers between devices with their start and end apart: 2, of which 2 were waited for; matrix products, arithmetic and copies ran while one was open for 4% of the time, Pallas kernels for 0%

commit v1 on v0

--- a/solution.py
+++ b/solution.py
@@ -2,6 +2,24 @@
 import jax.numpy as jnp
 from jax import lax
 from jax.sharding import PartitionSpec as P
+
+
+def joined_along(blocks, dim):
+    blocks = jnp.moveaxis(blocks, 0, dim)
+    lengths = blocks.shape
+    return blocks.reshape(*lengths[:dim], lengths[dim] * lengths[dim + 1], *lengths[dim + 2 :])
+
+
+def collected_by_bits(x, axis):
+    size = lax.axis_size(axis)
+    blocks = x[None]
+    for level in range(size.bit_length() - 1):
+        bit = 1 << level
+        partner_block = lax.ppermute(blocks, axis, [(i, i ^ bit) for i in range(size)])
+        both = jnp.stack([blocks, partner_block])
+        upper = lax.axis_index(axis) >> level & 1
+        blocks = jnp.where(upper == 0, both, both[::-1]).reshape(-1, *x.shape)
+    return blocks
 
 
 def on_device(amps, fitted, screen, owner, eps_occ, eps_vir):
@@ -35,7 +53,7 @@
     )
     denominator = virt_pair - eps_share[:, None, None, None]
     divided = (cycle_share / denominator).astype(jnp.bfloat16)
-    gathered = lax.all_gather(divided, "aux", axis=0, tiled=True)
+    gathered = joined_along(collected_by_bits(divided, "aux"), 0)
     return gathered[:occ_rows]
 
 

time: 68.6 us -> 66.2 us (0.965)
  blocking collectives: 13.8 us -> 0 us
  waiting for transfers between devices: 22 us -> 32 us
  other arithmetic: 3.36 us -> 4.37 us
  starting transfers between devices: 5.37 us -> 6.24 us
    all_gather x1 -> x0, blocking collectives: 13.8 us -> none  [on_device(): gathered = lax.all_gather(divided, 'aux', axis=0, tiled=True)]
    ppermute x0 -> x2, waiting for transfers between devices: none -> 10.1 us  [collected_by_bits(): lax.ppermute(blocks, axis, [(i, i ^ bit) for i in range(size)])]
    broadcast_in_dim x0 -> x1, other arithmetic: none -> 1.07 us  [collected_by_bits(): blocks = x[None]]
    convert_element_type x1 -> x0, other arithmetic: 1 us -> none  [on_device(): divided = (cycle_share / denominator).astype(jnp.bfloat16)]
    ppermute x0 -> x2, starting transfers between devices: none -> 0.87 us  [collected_by_bits(): lax.ppermute(blocks, axis, [(i, i ^ bit) for i in range(size)])]
    select_n x0 -> x1, other arithmetic: none -> 0.76 us  [collected_by_bits(): blocks = jnp.where(upper == 0, both, both[::-1]).reshape(-1, *x.shape)]
    unnamed x13 -> x14, local copies, waits for them, and re-layouts: 2.19 us -> 1.49 us
  transfers between devices with their start and end apart: 2 -> 4, of which waited for: 2 -> 4; matrix products, arithmetic and copies ran while one was open for 4% -> 4% of each run, Pallas kernels for 0% -> 0%
where the time goes in v1:
time: 66.2 us; the launch traced here: 65.8 us
  waiting for transfers between devices  32 us (48%)
  between operations  16.1 us (24%)
  starting transfers between devices  6.24 us (9%)
  other arithmetic  4.37 us (7%)
  local copies, waits for them, and re-layouts  4.08 us (6%)
  matrix products  3.05 us (5%)
    reduce_scatter x1, waiting for transfers between devices, on_device(): lax.psum_scatter(padded, 'aux', scatter_dimension=0, tiled=True)  16.3 us
    ppermute x2, waiting for transfers between devices, collected_by_bits(): lax.ppermute(blocks, axis, [(i, i ^ bit) for i in range(size)])  10.1 us
    all_to_all x1, waiting for transfers between devices, on_device(): lax.all_to_all(permuted, 'tile', split_axis=1, concat_axis=0, tiled=True)  5.5 us
    all_to_all x1, starting transfers between devices, on_device(): lax.all_to_all(permuted, 'tile', split_axis=1, concat_axis=0, tiled=True)  5.33 us
    dot_general x1, matrix products, on_device(): jnp.einsum('qia,qpb->iapb', screened, intermed, preferred_element_type=jn...  3.05 us
    select_n x2, other arithmetic, on_device(): permuted = jnp.take(amps, owner, axis=1)  1.56 us
    unnamed x14, local copies, waits for them, and re-layouts  1.49 us
  transfers between devices with their start and end apart: 4, of which 4 were waited for; matrix products, arithmetic and copies ran while one was open for 4% of the time, Pallas kernels for 0%

profile of v1, /device:TPU:0, one launch (start us, length us, event | category | flops | bytes accessed | tf_op | source)
XLA Modules:
  0.0 65.8 jit_solution(2126069452990933894)
XLA Ops:
  6.5 0.0 copy-start
  6.5 0.0 copy-start.5
  6.5 0.0 copy-start.1
  6.5 0.8 %compare_select_fusion = s32[8]{0:T(128)S(1)} fusion(s32[8]{0:T(128)} %param.9), kind=kLoop, calls=%fused_computation.17 | loop fusion | flops 24 | bytes 64 | tf_op jit(solution)/shard_map/jit(_take)/jit(_where)/select_n | solution.py:30
  7.3 0.0 copy-done.5
  7.3 0.2 copy-done
  7.5 0.6 gather_fusion
  8.1 0.8 %bitcast_select_fusion = bf16[1,8,128,128]{3,2,0,1:T(8,128)(2,1)} fusion(bf16[8,128,128]{2,1,0:T(8,128)(2,1)S(1)} %gather_fusion, pred[8]{0:T(512)(128)(4,1)S(1)} %compare_and_fusion), kind=kLoop, calls=%fused_computation.9 | loop fusion | flops 131072 | bytes 524296 | tf_op jit(solution)/shard_map/jit(_take)/select_n | solution.py:30
  8.9 0.0 copy-start.4
  8.9 5.3 %all-to-all-start = ((bf16[1,8,128,128]{3,2,0,1:T(8,128)(2,1)}), bf16[1,8,128,128]{3,2,0,1:T(8,128)(2,1)}, u32[]{:S(2)}, u32[]{:S(2)}) async-start(bf16[1,8,128,128]{3,2,0,1:T(8,128)(2,1)} %bitcast_select_fusion), calls=%async_computation | async-start | bytes 524288 | tf_op jit(solution)/shard_map/all_to_all | solution.py:31
  14.2 0.0 reduce-scatter.2.cloned.1.call-start
  14.3 0.0 copy-done.4
  14.3 0.0 copy-done.1
  14.3 0.7 %broadcast_multiply_fusion = bf16[512,8,128]{2,1,0:T(8,128)(2,1)S(1)} fusion(bf16[512,8,128]{2,1,0:T(8,128)(2,1)S(1)} %copy-done.1, bf16[512,8]{1,0:T(8,128)(2,1)S(1)} %bitcast.40), kind=kLoop, calls=%fused_computation.5 | loop fusion | flops 524288 | bytes 2105344 | tf_op jit(solution)/shard_map/mul | solution.py:29
  15.1 0.7 %copy.9 = bf16[512,8,128]{0,2,1:T(8,128)(2,1)S(1)} copy(bf16[512,8,128]{2,1,0:T(8,128)(2,1)S(1)} %broadcast_multiply_fusion) | data formatting | bytes 2097152 | tf_op jit(solution)/shard_map/mul | solution.py:29
  15.7 5.5 %all-to-all-done = bf16[1,8,128,128]{3,2,0,1:T(8,128)(2,1)} async-done(((bf16[1,8,128,128]{3,2,0,1:T(8,128)(2,1)}), bf16[1,8,128,128]{3,2,0,1:T(8,128)(2,1)}, u32[]{:S(2)}, u32[]{:S(2)}) %all-to-all-start) | async-done | bytes 262176 | tf_op jit(solution)/shard_map/all_to_all | solution.py:31
  21.2 3.1 %convolution_bitcast_fusion = f32[8,128,1,128]{3,1,0,2:T(8,128)} fusion(bf16[512,8,128]{0,2,1:T(8,128)(2,1)S(1)} %copy.9, bf16[1,8,128,128]{3,2,0,1:T(8,128)(2,1)} %all-to-all-done), kind=kOutput, calls=%fused_computation.1 | convolution fusion | flops 268500992 | bytes 1835008 | tf_op jit(solution)/shard_map/qia,qpb->iapb/dot_general | solution.py:35
  24.3 0.0 reduce-scatter.2.cloned.1.call-update
  24.3 0.6 dynamic_slice.6
  26.9 0.0 copy-start.6
  26.9 0.6 copy-done.6
  27.5 0.1 dynamic_slice.7
  27.6 0.6 dynamic-slice.2
  28.9 0.0 copy-start.3
  28.9 0.6 copy-done.3
  29.5 0.1 add_subtract_fusion
  29.6 16.3 %reduce-scatter.2.cloned.1.call-done = f32[2,128,1,128]{3,1,0,2:T(8,128)} async-done(((f32[8,128,1,128]{3,1,0,2:T(8,128)}), f32[2,128,1,128]{3,1,0,2:T(8,128)}) %reduce-scatter.2.cloned.1.call-update) | async-done | bytes 131088 | tf_op jit(solution)/shard_map/reduce_scatter | solution.py:49
  45.9 0.0 copy-start.2
  45.9 1.1 %fusion.9 = bf16[1,2,128,1,128]{4,2,1,3,0:T(8,128)(2,1)S(1)} fusion(f32[2,128,1,128]{3,1,0,2:T(8,128)} %reduce-scatter.2.cloned.1.call-done, f32[2]{0:T(128)S(1)} %dynamic_slice.7, f32[128,128]{1,0:T(8,128)S(1)} %add_subtract_fusion), kind=kLoop, calls=%fused_computation.20 | loop fusion | flops 98304 | bytes 262152 | tf_op jit(solution)/shard_map/broadcast_in_dim | solution.py:15
  47.0 0.1 collective-permute-start
  47.1 0.0 copy-done.2
  47.1 0.1 fusion.8
  47.2 4.1 %collective-permute-done = bf16[1,2,128,1,128]{4,2,1,3,0:T(8,128)(2,1)S(1)} collective-permute-done((bf16[1,2,128,1,128]{4,2,1,3,0:T(8,128)(2,1)S(1)}, bf16[1,2,128,1,128]{4,2,1,3,0:T(8,128)(2,1)S(1)}, u32[]{:S(2)}, u32[]{:S(2)}) %collective-permute-start) | collective-permute-done | bytes 65568 | tf_op jit(solution)/shard_map/ppermute | solution.py:18
  51.4 0.8 %collective-permute-start.1 = (bf16[2,2,128,1,128]{4,2,1,0,3:T(8,128)(2,1)S(1)}, bf16[2,2,128,1,128]{4,2,1,0,3:T(8,128)(2,1)S(1)}, u32[]{:S(2)}, u32[]{:S(2)}) collective-permute-start(bf16[2,2,128,1,128]{4,2,1,0,3:T(8,128)(2,1)S(1)} %get-tuple-element.17), channel_id=1, source_target_pairs={{0,2},{1,3},{2,0},{3,1},{4,6},{5,7},{6,4},{7,5},{8,10},{9,11},{10,... | collective-permute-start | bytes 393224 | tf_op jit(solution)/shard_map/ppermute | solution.py:18
  52.2 6.0 %collective-permute-done.1 = bf16[2,2,128,1,128]{4,2,1,0,3:T(8,128)(2,1)S(1)} collective-permute-done((bf16[2,2,128,1,128]{4,2,1,0,3:T(8,128)(2,1)S(1)}, bf16[2,2,128,1,128]{4,2,1,0,3:T(8,128)(2,1)S(1)}, u32[]{:S(2)}, u32[]{:S(2)}) %collective-permute-start.1) | collective-permute-done | bytes 131104 | tf_op jit(solution)/shard_map/ppermute | solution.py:18
  58.2 0.8 %reverse_select_fusion = bf16[2,2,2,128,1,128]{5,3,2,1,4,0:T(8,128)(2,1)} fusion(bf16[2,2,2,128,1,128]{5,3,2,1,4,0:T(8,128)(2,1)S(1)} %pad_maximum_fusion, pred[]{:T(512)S(6)} %eq.6), kind=kLoop, calls=%fused_computation.6 | loop fusion | flops 131072 | bytes 524289 | tf_op jit(solution)/shard_map/jit(_where)/select_n | solution.py:21
  (7 shorter events, 0.1 us)
Async XLA Ops:
  6.5 1.0 %copy-start = (bf16[1,8,128,128]{3,2,1,0:T(8,128)(2,1)S(1)}, bf16[1,8,128,128]{3,2,1,0:T(8,128)(2,1)}, u32[]{:S(2)}) copy-start(bf16[1,8,128,128]{3,2,1,0:T(8,128)(2,1)} %param.6) | copy-start | bytes 786436
  6.5 0.8 %copy-start.5 = (s32[8]{0:T(128)S(1)}, s32[8]{0:T(128)}, u32[]{:S(2)}) copy-start(s32[8]{0:T(128)} %param.9) | copy-start | bytes 100
  6.5 7.8 %copy-start.1 = (bf16[512,8,128]{2,1,0:T(8,128)(2,1)S(1)}, bf16[512,8,128]{2,1,0:T(8,128)(2,1)}, u32[]{:S(2)}) copy-start(bf16[512,8,128]{2,1,0:T(8,128)(2,1)} %param.7) | copy-start | bytes 3145732
  8.9 5.4 %copy-start.4 = (s32[4,8]{1,0:T(4,128)S(1)}, s32[4,8]{1,0:T(4,128)}, u32[]{:S(2)}) copy-start(s32[4,8]{1,0:T(4,128)} %param.8) | copy-start | bytes 388
  8.9 12.3 %all-to-all-start = ((bf16[1,8,128,128]{3,2,0,1:T(8,128)(2,1)}), bf16[1,8,128,128]{3,2,0,1:T(8,128)(2,1)}, u32[]{:S(2)}, u32[]{:S(2)}) async-start(bf16[1,8,128,128]{3,2,0,1:T(8,128)(2,1)} %bitcast_select_fusion), calls=%async_computation | async-start | bytes 524288 | tf_op jit(solution)/shard_map/all_to_all | solution.py:31
  14.2 31.7 %reduce-scatter.2.cloned.1.call-start = ((), (), s32[]{:S(2)}) async-start(), calls=%async_computation.2 | async-start | bytes 655360 | tf_op jit(solution)/shard_map/reduce_scatter | solution.py:49
  26.9 0.7 %copy-start.6 = (f32[8]{0:T(128)S(1)}, f32[8]{0:T(128)}, u32[]{:S(2)}) copy-start(f32[8]{0:T(128)} %param.10) | copy-start | bytes 100
  28.9 0.7 %copy-start.3 = (f32[128]{0:T(128)S(1)}, f32[128]{0:T(128)}, u32[]{:S(2)}) copy-start(f32[128]{0:T(128)} %param.11) | copy-start | bytes 1540
  45.9 1.2 %copy-start.2 = (f32[2,128,1,128]{3,1,0,2:T(8,128)S(1)}, f32[2,128,1,128]{3,1,0,2:T(8,128)}, u32[]{:S(2)}) copy-start(f32[2,128,1,128]{3,1,0,2:T(8,128)} %reduce-scatter.2.cloned.1.call-done) | copy-start | bytes 393220
  47.0 4.3 %collective-permute-start = (bf16[1,2,128,1,128]{4,2,1,3,0:T(8,128)(2,1)S(1)}, bf16[1,2,128,1,128]{4,2,1,3,0:T(8,128)(2,1)S(1)}, u32[]{:S(2)}, u32[]{:S(2)}) collective-permute-start(bf16[1,2,128,1,128]{4,2,1,3,0:T(8,128)(2,1)S(1)} %fusion.9), channel_id=1, source_target_pairs={{0,1},{1,0},{2,3},{3,2},{4,5},{5,4},{6,7},{7,6},{8,9},{9,8},{10,11... | collective-permute-start | bytes 196616 | tf_op jit(solution)/shard_map/ppermute | solution.py:18
  51.4 6.8 %collective-permute-start.1 = (bf16[2,2,128,1,128]{4,2,1,0,3:T(8,128)(2,1)S(1)}, bf16[2,2,128,1,128]{4,2,1,0,3:T(8,128)(2,1)S(1)}, u32[]{:S(2)}, u32[]{:S(2)}) collective-permute-start(bf16[2,2,128,1,128]{4,2,1,0,3:T(8,128)(2,1)S(1)} %get-tuple-element.17), channel_id=1, source_target_pairs={{0,2},{1,3},{2,0},{3,1},{4,6},{5,7},{6,4},{7,5},{8,10},{9,11},{10,... | collective-permute-start | bytes 393224 | tf_op jit(solution)/shard_map/ppermute | solution.py:18
Sparse Core Ops, SparseCore 0:
  24.4 21.4 reduce-scatter.1
